TPU v7x, 128 devices: a whole 4x4x4 slice. The times are simulated.
128 devices in a mesh: group: 8 (over z, core), member: 16 (over x, y).
Axes of the slice: x: 4, y: 4, z: 4, core: 2. Of those that a mesh axis runs over, the one named last changes fastest.
Arguments:
- hidden: bfloat16 [12288, 2048], P('group'), may hold values from -6 to 6
- token_slab: int32 [12288, 1], P(('group', 'member')), may hold values from 0 to 127; in each aligned block of 96 rows (0 to 95, 96 to 191, ...) at most 2 rows name the same one
- token_row: int32 [12288], P(('group', 'member')), may hold values from 0 to 2047
- slab_owner: int32 [128], replicated, may hold values from 0 to 127, each once
- ple_table: bfloat16 [262144, 256], P(('group', 'member')), may hold values from -0.375 to 0.375
- norm_gains: float32 [1, 3, 2048], replicated, may hold values from 0.1 to 1.9
- w_gate: bfloat16 [1, 2048, 8192], P(None, None, 'member'), may hold values from -0.125 to 0.125
- w_up: bfloat16 [1, 2048, 8192], P(None, None, 'member'), may hold values from -0.125 to 0.125
- w_down: bfloat16 [1, 8192, 2048], P(None, 'member'), may hold values from -0.0625 to 0.0625
- ple_gate: bfloat16 [1, 2048, 256], P(None, None, 'member'), may hold values from -0.125 to 0.125
- ple_proj: bfloat16 [1, 256, 2048], P(None, 'member'), may hold values from -0.375 to 0.375
Outputs:
- hidden_out: bfloat16 [12288, 2048], P('group')
Inputs may be any that keep to these rules, and one draw needn't show every extreme that they name: Within the 96 tokens of one device (aligned blocks of token_slab), no slab is named by more than 2 tokens. Each number appears once: slab s is stored in rows slab_owner[s] * 2048 to slab_owner[s] * 2048 + 2047 of ple_table.
All inputs are finite; a program needn't handle non-finite values.
Results may differ from a plain program's by a relative error of at most 0.0061.
Values may be sent and summed in bfloat16 or wider, within the bound.
A program may use at most 128 MiB of HBM per device.

v0:
```python
import jax
import jax.numpy as jnp
from jax import lax
from jax.sharding import PartitionSpec as P

PLE = 256
epsilon = 1e-06


def in_blocks(x, dim, devices):
    shape = x.shape
    parts = x.reshape(*shape[:dim], devices, shape[dim] // devices, *shape[dim + 1 :])
    return jnp.moveaxis(parts, dim, 0)


def joined_along(parts, dim):
    shape = list(parts.shape[1:])
    shape[dim] *= parts.shape[0]
    return jnp.moveaxis(parts, 0, dim).reshape(shape)


def exchange_both(x, axis, axes, splits, concats):
    sizes = [lax.axis_size(a) for a in axes]
    parts = in_blocks(x, splits[0], sizes[0])
    parts = jnp.moveaxis(in_blocks(parts, splits[1] + 1, sizes[1]), 0, 1)
    inside = parts.shape[2:]
    parts = parts.reshape(-1, *inside)
    parts = lax.all_to_all(parts, axis, split_axis=0, concat_axis=0, tiled=True)
    parts = joined_along(parts.reshape(*sizes, *inside), concats[0] + 1)
    return joined_along(parts, concats[1])


def norm_rows(values, scales):
    return values * lax.rsqrt(jnp.mean(values * values, axis=-1, keepdims=True) + epsilon) * scales


def lookup_rows(wanted, ple_table):
    flat_ids = wanted.reshape(-1) - 1
    one_hot = (
        flat_ids[:, None] == jnp.arange(ple_table.shape[0], dtype=jnp.int32)[None, :]
    ).astype(jnp.bfloat16)
    served = jnp.dot(one_hot, ple_table, preferred_element_type=jnp.float32).astype(jnp.bfloat16)
    return served.reshape(wanted.shape + (ple_table.shape[1],))


def request_slots(slab_ids, token_row, slab_owner, devices, slots):
    target = slab_owner[slab_ids]
    order = jnp.arange(token_row.shape[0], dtype=jnp.int32)
    earlier = (target[None, :] == target[:, None]) & (order[None, :] < order[:, None])
    slot_of = jnp.sum(earlier.astype(jnp.int32), axis=1)
    hit_map = (target[:, None, None] == jnp.arange(devices, dtype=jnp.int32)[None, :, None]) & (
        slot_of[:, None, None] == jnp.arange(slots, dtype=jnp.int32)[None, None, :]
    )
    requests = jnp.sum(jnp.where(hit_map, token_row[:, None, None] + 1, 0), axis=0)
    return (hit_map, requests)


def pick_rows(hit_map, returned):
    return jnp.einsum(
        "tdc,dcw->tw", hit_map.astype(jnp.bfloat16), returned, preferred_element_type=jnp.float32
    ).astype(jnp.bfloat16)


def combine_branch(current, partial_value, scales):
    summed = lax.psum(partial_value, "member")
    return current + norm_rows(summed, scales)


def per_device(
    hidden,
    token_slab,
    token_row,
    slab_owner,
    ple_table,
    norm_gains,
    w_gate,
    w_up,
    w_down,
    ple_gate,
    ple_proj,
):
    members = lax.axis_size("member")
    devices = lax.axis_size("group") * members
    tokens_here = token_row.shape[0]
    slots = max(2, (2 * tokens_here + devices - 1) // devices)
    slab_ids = token_slab[:, 0]
    hit_map, requests = request_slots(slab_ids, token_row, slab_owner, devices, slots)
    grouped = requests.reshape(lax.axis_size("group"), members, slots)
    received = lax.all_to_all(
        lax.all_to_all(grouped, "group", split_axis=0, concat_axis=0, tiled=True),
        "member",
        split_axis=1,
        concat_axis=1,
        tiled=True,
    )
    served = lookup_rows(received, ple_table)
    returned = exchange_both(served, ("group", "member"), ("group", "member"), (0, 1), (0, 1))
    own_rows = pick_rows(hit_map, returned.reshape(devices, slots, ple_table.shape[1]))
    per_member = ple_gate.shape[2]
    layers = w_gate.shape[0]
    pieces = own_rows.reshape(tokens_here, layers, members, per_member)
    columns = lax.all_to_all(pieces, "member", split_axis=2, concat_axis=0, tiled=True)
    ple_part = columns.reshape(-1, layers, per_member).astype(jnp.float32) * PLE**0.5
    current = hidden.astype(jnp.float32)
    normed = norm_rows(current, norm_gains[0, 0]).astype(jnp.bfloat16)
    gate_part = jnp.dot(normed, w_gate[0], preferred_element_type=jnp.float32)
    up_part = jnp.dot(normed, w_up[0], preferred_element_type=jnp.float32)
    activated = (jax.nn.gelu(gate_part, approximate=True) * up_part).astype(jnp.bfloat16)
    mlp_out = jnp.dot(activated, w_down[0], preferred_element_type=jnp.float32)
    current = combine_branch(current, mlp_out, norm_gains[0, 1])
    current_b = current.astype(jnp.bfloat16)
    ple_gate_out = jnp.dot(current_b, ple_gate[0], preferred_element_type=jnp.float32)
    ple_act = (jax.nn.gelu(ple_gate_out, approximate=True) * ple_part[:, 0, :]).astype(jnp.bfloat16)
    ple_out = jnp.dot(ple_act, ple_proj[0], preferred_element_type=jnp.float32)
    current = combine_branch(current, ple_out, norm_gains[0, 2])
    return current.astype(jnp.bfloat16)


def solution(mesh):
    return jax.shard_map(
        per_device,
        mesh=mesh,
        in_specs=(
            P("group", None),
            P(("group", "member"), None),
            P(("group", "member")),
            P(),
            P(("group", "member"), None),
            P(),
            P(None, None, "member"),
            P(None, None, "member"),
            P(None, "member", None),
            P(None, None, "member"),
            P(None, "member", None),
        ),
        out_specs=P("group", None),
        check_vma=False,
    )
```

profile of v0, /device:TPU:1, one launch (start us, length us, event | category | flops | bytes accessed | tf_op | source)
XLA Modules:
  0.0 437.7 jit_solution(8497324638105972487)
XLA Ops:
  6.5 0.0 copy-start
  6.5 0.0 copy-start.7
  6.5 0.0 all-reduce.3.cloned.1.call-start
  6.5 0.0 copy-start.3
  6.5 4.2 fusion
  10.8 0.0 copy-done.7
  10.8 0.5 copy-done.3
  11.3 6.8 %fusion.17 = f32[1536,512]{1,0:T(8,128)} fusion(bf16[1,2048,512]{2,1,0:T(8,128)(2,1)} %param.17, bf16[1536,2048]{1,0:T(8,128)(2,1)S(1)} %copy-done.3, f32[2048]{0:T(1024)S(1)} %bitcast.58, f32[1536]{0:T(1024)S(1)} %add_rsqrt_fusion.2), kind=kOutput, calls=%fused_computation.25 | convolution fusion | flops 3233808384 | bytes 11548672 | tf_op jit(solution)/shard_map/dot_general | solution.py:106
  18.1 0.0 copy-done
  18.1 13.3 %fusion.14 = f32[1536,2048]{1,0:T(8,128)} fusion(bf16[1,512,2048]{2,1,0:T(8,128)(2,1)S(1)} %copy-done, f32[1536,512]{1,0:T(8,128)} %fusion.17, bf16[1,2048,512]{2,1,0:T(8,128)(2,1)} %param.18, bf16[1536,2048]{1,0:T(8,128)(2,1)} %param.11, f32[2048]{0:T(1024)S(1)} %bitcast.59, f32[1536]{0:T(1024)S(1)} %add_rsqrt_fusion.2), kind=kOutput, calls=%fused_computation.22 | convolution fusion | flops 6462898176 | bytes 26228736 | tf_op jit(solution)/shard_map/dot_general | solution.py:109
  31.4 0.0 copy-start.9
  31.4 0.0 copy-start.2
  31.4 0.0 copy-start.10
  31.4 0.0 copy-start.8
  31.4 0.0 all-reduce.3.cloned.1.call-update
  31.4 0.0 all-reduce.5.cloned.1.call-start
  31.5 0.6 copy-done.9
  32.1 0.0 copy-done.2
  32.1 1.2 gather_fusion
  33.3 0.2 convert_reduce_fusion
  33.5 0.0 copy-done.10
  33.5 0.1 iota_compare_fusion.5
  33.6 0.1 fusion.30
  33.7 0.1 reshape.110
  33.8 11.2 %all_to_all.24 = s32[8,16,2]{1,2,0:T(2,128)S(1)} all-to-all(s32[8,16,2]{1,2,0:T(2,128)S(1)} %copy.33), channel_id=1, replica_groups=mesh['group'=8,'member'=16] {'group'}, dimensions={0} | all-to-all | bytes 2048 | tf_op jit(solution)/shard_map/all_to_all | solution.py:90
  45.0 0.1 copy.34
  45.1 13.2 %all_to_all.25 = s32[8,16,2]{0,2,1:T(2,128)S(1)} all-to-all(s32[8,16,2]{0,2,1:T(2,128)S(1)} %copy.34), channel_id=1, replica_groups=mesh['group'=8,'member'=16] {'member'}, dimensions={1} | all-to-all | bytes 2048 | tf_op jit(solution)/shard_map/all_to_all | solution.py:89
  58.3 0.1 copy.35
  58.4 0.1 copy.36
  58.5 0.1 sub.7
  58.7 0.0 copy-done.8
  58.7 0.5 fusion.26
  59.2 0.1 reshape_transpose_transpose_reshape_reshape_reshape.3
  59.2 16.6 %all_to_all.26 = bf16[128,1,1,2,256]{4,3,2,1,0:T(2,128)(2,1)S(1)} all-to-all(bf16[128,1,1,2,256]{4,3,2,1,0:T(2,128)(2,1)S(1)} %bitcast.52), channel_id=1, replica_groups=mesh['group'=8,'member'=16] {'group','member'}, dimensions={0} | all-to-all | bytes 262144 | tf_op jit(solution)/shard_map/all_to_all | solution.py:28
  75.8 0.2 fusion.27
  76.1 0.1 copy.39
  76.2 10.0 %all_to_all.27 = bf16[96,1,16,16]{0,3,1,2:T(8,128)(2,1)S(1)} all-to-all(bf16[96,1,16,16]{0,3,1,2:T(8,128)(2,1)S(1)} %bitcast.54), channel_id=1, replica_groups=mesh['group'=8,'member'=16] {'member'}, dimensions={2} | all-to-all | bytes 98304 | tf_op jit(solution)/shard_map/all_to_all | solution.py:102
  86.2 0.1 mul.160
  86.3 0.0 copy-start.5
  86.3 0.0 copy-start.6
  86.4 129.4 %all-reduce.3.cloned.1.call-done = f32[1536,2048]{1,0:T(8,128)} async-done(((f32[1536,2048]{1,0:T(8,128)}), f32[1536,2048]{1,0:T(8,128)}) %all-reduce.3.cloned.1.call-update) | async-done | bytes 12582928 | tf_op jit(solution)/shard_map/psum | solution.py:65
  215.7 5.5 %multiply_reduce_fusion.1 = f32[1536]{0:T(1024)S(1)} fusion(f32[1536,2048]{1,0:T(8,128)} %all-reduce.3.cloned.1.call-done), kind=kLoop, calls=%fused_computation.9 | loop fusion | flops 6289920 | bytes 12589056 | tf_op jit(solution)/shard_map/reduce_sum | solution.py:34
  221.2 0.0 copy-done.5
  221.2 0.0 copy-done.6
  221.2 11.5 %fusion.47 = f32[1536,2048]{1,0:T(8,128)} fusion(f32[1536,16]{0,1:T(8,128)S(1)} %mul.160, f32[1536,2048]{1,0:T(8,128)} %all-reduce.3.cloned.1.call-done, bf16[1536,2048]{1,0:T(8,128)(2,1)} %param.11, f32[2048]{0:T(1024)S(1)} %bitcast.55, f32[1536]{0:T(1024)S(1)} %add_rsqrt_fusion.1, bf16[1,16,2048]{2,1,0:T(8,128)(2,1)S(1)} %copy-done.5, ...), kind=kOutput, calls=%fused_computation.47 | convolution fusion | flops 217300992 | bytes 31700992 | tf_op jit(solution)/shard_map/dot_general | solution.py:114
  232.8 0.0 all-reduce.5.cloned.1.call-update
  232.8 178.6 %all-reduce.5.cloned.1.call-done = f32[1536,2048]{1,0:T(8,128)} async-done(((f32[1536,2048]{1,0:T(8,128)}), f32[1536,2048]{1,0:T(8,128)}) %all-reduce.5.cloned.1.call-update) | async-done | bytes 12582928 | tf_op jit(solution)/shard_map/psum | solution.py:65
  411.4 0.0 copy-start.4
  411.4 5.6 %multiply_reduce_fusion = f32[1536]{0:T(1024)S(1)} fusion(f32[1536,2048]{1,0:T(8,128)} %all-reduce.5.cloned.1.call-done), kind=kLoop, calls=%fused_computation.8 | loop fusion | flops 6289920 | bytes 12589056 | tf_op jit(solution)/shard_map/reduce_sum | solution.py:34
  417.1 2.5 copy-done.4
  419.6 0.0 copy-start.1
  419.6 11.3 %add_convert_fusion = bf16[1536,2048]{1,0:T(8,128)(2,1)} fusion(f32[1536,2048]{1,0:T(8,128)S(1)} %copy-done.4, f32[1536,2048]{1,0:T(8,128)} %all-reduce.3.cloned.1.call-done, bf16[1536,2048]{1,0:T(8,128)(2,1)} %param.11, f32[2048]{0:T(1024)S(1)} %bitcast.57, f32[1536]{0:T(1024)S(1)} %add_rsqrt_fusion, f32[2048]{0:T(1024)S(1)} %bitcast.56, ...), kind=kLoop, calls=%fused_computation.7 | loop fusion | flops 25165824 | bytes 37777408 | tf_op jit(solution)/shard_map/convert_element_type | solution.py:116
  430.9 0.0 copy-done.1
  (13 shorter events, 0.1 us)
Async XLA Ops:
  6.5 11.6 %copy-start = (bf16[1,512,2048]{2,1,0:T(8,128)(2,1)S(1)}, bf16[1,512,2048]{2,1,0:T(8,128)(2,1)}, u32[]{:S(2)}) copy-start(bf16[1,512,2048]{2,1,0:T(8,128)(2,1)} %param.19) | copy-start | bytes 6291460
  6.5 4.3 copy-start.7
  6.5 209.2 %all-reduce.3.cloned.1.call-start = ((), (), s32[]{:S(2)}) async-start(), calls=%async_computation.4 | async-start | bytes 25165824 | tf_op jit(solution)/shard_map/psum | solution.py:65
  6.5 4.8 %copy-start.3 = (bf16[1536,2048]{1,0:T(8,128)(2,1)S(1)}, bf16[1536,2048]{1,0:T(8,128)(2,1)}, u32[]{:S(2)}) copy-start(bf16[1536,2048]{1,0:T(8,128)(2,1)} %param.11) | copy-start | bytes 18874372
  31.4 0.7 copy-start.9
  31.4 0.7 copy-start.2
  31.4 2.1 copy-start.10
  31.4 27.3 %copy-start.8 = (bf16[2048,256]{1,0:T(8,128)(2,1)S(1)}, bf16[2048,256]{1,0:T(8,128)(2,1)}, u32[]{:S(2)}) copy-start(bf16[2048,256]{1,0:T(8,128)(2,1)} %param.15) | copy-start | bytes 3145732
  31.4 380.0 %all-reduce.5.cloned.1.call-start = ((), (), s32[]{:S(2)}) async-start(), calls=%async_computation.5 | async-start | bytes 25165824 | tf_op jit(solution)/shard_map/psum | solution.py:65
  86.3 134.9 %copy-start.5 = (bf16[1,16,2048]{2,1,0:T(8,128)(2,1)S(1)}, bf16[1,16,2048]{2,1,0:T(8,128)(2,1)}, u32[]{:S(2)}) copy-start(bf16[1,16,2048]{2,1,0:T(8,128)(2,1)} %param.21) | copy-start | bytes 196612
  86.3 134.9 %copy-start.6 = (bf16[1,2048,16]{1,2,0:T(8,128)(2,1)S(1)}, bf16[1,2048,16]{1,2,0:T(8,128)(2,1)}, u32[]{:S(2)}) copy-start(bf16[1,2048,16]{1,2,0:T(8,128)(2,1)} %param.20) | copy-start | bytes 196612
  411.4 8.2 %copy-start.4 = (f32[1536,2048]{1,0:T(8,128)S(1)}, f32[1536,2048]{1,0:T(8,128)}, u32[]{:S(2)}) copy-start(f32[1536,2048]{1,0:T(8,128)} %all-reduce.5.cloned.1.call-done) | copy-start | bytes 37748740
  419.6 11.3 %copy-start.1 = (bf16[1,512,2048]{2,1,0:T(8,128)(2,1)S(1)}, bf16[1,512,2048]{2,1,0:T(8,128)(2,1)}, u32[]{:S(2)}) copy-start(bf16[1,512,2048]{2,1,0:T(8,128)(2,1)} %param.19) | copy-start | bytes 6291460
Sparse Core Ops, SparseCore 0:
  31.6 184.1 all-reduce.2
  232.9 178.4 all-reduce.4
where the time goes:
time: 438 us
  waiting for transfers between devices  308 us (70%)
  blocking collectives  51 us (12%)
  matrix products  32.3 us (7%)
  other arithmetic  27 us (6%)
  between operations  13.6 us (3%)
  local copies, waits for them, and re-layouts  5.69 us (1%)
    psum x2, waiting for transfers between devices, combine_branch(): summed = lax.psum(partial_value, 'member')  308 us
    all_to_all x1, blocking collectives, exchange_both(): parts = lax.all_to_all(parts, axis, split_axis=0, concat_axis=0, tiled=True)  16.6 us
    reduce_sum x3, other arithmetic, norm_rows(): jnp.mean(values * values, axis=-1, keepdims=True) + epsilon  15.3 us
    dot_general x1, matrix products, per_device(): mlp_out = jnp.dot(activated, w_down[0], preferred_element_type=jnp.float32)  13.3 us
    all_to_all x1, blocking collectives, per_device(): lax.all_to_all(lax.all_to_all(grouped, 'group', split_axis=0, concat_axis...  13.2 us
    dot_general x1, matrix products, per_device(): ple_out = jnp.dot(ple_act, ple_proj[0], preferred_element_type=jnp.float32)  11.5 us
    convert_element_type x1, other arithmetic, per_device(): return current.astype(jnp.bfloat16)  11.3 us
    all_to_all x1, blocking collectives, per_device(): lax.all_to_all(grouped, 'group', split_axis=0, concat_axis=0, tiled=True)  11.2 us
  transfers between devices with their start and end apart: 2, of which 2 were waited for; matrix products, arithmetic and copies ran while one was open for 1% of the time, Pallas kernels for 0%

commit v1 on v0

--- a/solution.py
+++ b/solution.py
@@ -62,7 +62,9 @@
 
 
 def combine_branch(current, partial_value, scales):
-    summed = lax.psum(partial_value, "member")
+    summed = partial_value
+    for hop in (1, 2, 4, 8):
+        summed = summed + lax.ppermute(summed, "member", [(dev, dev ^ hop) for dev in range(16)])
     return current + norm_rows(summed, scales)
 
 

time: 438 us -> 2320 us (5.30)
  waiting for transfers between devices: 308 us -> 1880 us
  blocking collectives: 51 us -> 300 us
  other arithmetic: 27 us -> 86.9 us
    ppermute x0 -> x8, waiting for transfers between devices: none -> 1880 us  [combine_branch(): lax.ppermute(summed, 'member', [(dev, dev ^ hop) for dev in range(16)])]
    psum x2 -> x0, waiting for transfers between devices: 308 us -> none  [combine_branch(): summed = lax.psum(partial_value, 'member')]
    all_to_all x1, blocking collectives: 13.2 us -> 255 us  [per_device(): lax.all_to_all(lax.all_to_all(grouped, 'group', split_axis=0, concat_axis...]
    add x0 -> x6, other arithmetic: none -> 44.8 us  [combine_branch(): summed + lax.ppermute(summed, 'member', [(dev, dev ^ hop) for dev in rang...]
  transfers between devices with their start and end apart: 2 -> 8, of which waited for: 2 -> 7; matrix products, arithmetic and copies ran while one was open for 1% -> 0% of each run, Pallas kernels for 0% -> 0%
where the time goes in v1:
time: 2320 us
  waiting for transfers between devices  1880 us (81%)
  blocking collectives  300 us (13%)
  other arithmetic  86.9 us (4%)
  matrix products  34.1 us (1%)
    ppermute x8, waiting for transfers between devices, combine_branch(): lax.ppermute(summed, 'member', [(dev, dev ^ hop) for dev in range(16)])  1880 us
    all_to_all x1, blocking collectives, per_device(): lax.all_to_all(lax.all_to_all(grouped, 'group', split_axis=0, concat_axis...  255 us
  transfers between devices with their start and end apart: 8, of which 7 were waited for; matrix products, arithmetic and copies ran while one was open for 0% of the time, Pallas kernels for 0%

profile of v1, /device:TPU:1, one launch (start us, length us, event | category | flops | bytes accessed | tf_op | source)
XLA Modules:
  0.0 2317.1 jit_solution(16277484750303687362)
XLA Ops:
  0.0 0.0 copy-start
  0.0 4.2 fusion
  4.2 0.7 fusion.68
  5.0 8.6 fusion.17
  13.5 0.0 copy-done
  13.5 13.3 fusion.14
  26.9 2.1 collective-permute-start
  29.0 269.9 %collective-permute-done = f32[1536,2048]{1,0:T(8,128)S(1)} collective-permute-done((f32[1536,2048]{1,0:T(8,128)}, f32[1536,2048]{1,0:T(8,128)S(1)}, u32[]{:S(2)}, u32[]{:S(2)}) %collective-permute-start) | collective-permute-done | bytes 12582944 | tf_op jit(solution)/shard_map/ppermute | solution.py:67
  298.9 6.0 add.96
  304.9 3.2 collective-permute-start.1
  308.2 269.0 %collective-permute-done.1 = f32[1536,2048]{1,0:T(8,128)} collective-permute-done((f32[1536,2048]{1,0:T(8,128)S(1)}, f32[1536,2048]{1,0:T(8,128)}, u32[]{:S(2)}, u32[]{:S(2)}) %collective-permute-start.1) | collective-permute-done | bytes 12582944 | tf_op jit(solution)/shard_map/ppermute | solution.py:67
  577.2 6.0 add.97
  583.3 0.0 copy-start.7
  583.3 0.0 copy-start.2
  583.3 0.0 copy-start.8
  583.3 0.0 copy-start.6
  583.3 1.2 collective-permute-start.2
  584.6 268.3 %collective-permute-done.2 = f32[1536,2048]{1,0:T(8,128)S(1)} collective-permute-done((f32[1536,2048]{1,0:T(8,128)S(1)}, f32[1536,2048]{1,0:T(8,128)S(1)}, u32[]{:S(2)}, u32[]{:S(2)}) %collective-permute-start.2) | collective-permute-done | bytes 12582944 | tf_op jit(solution)/shard_map/ppermute | solution.py:67
  852.9 5.4 add.98
  858.3 2.5 collective-permute-start.3
  860.8 0.0 copy-done.7
  860.8 0.0 copy-done.2
  860.9 1.2 gather_fusion
  862.1 0.2 convert_reduce_fusion
  862.3 0.0 copy-done.8
  862.3 0.1 iota_compare_fusion.5
  862.4 0.1 fusion.30
  862.5 0.1 reshape.110
  862.6 13.8 all_to_all.24
  876.4 0.1 copy.34
  876.5 254.6 %all_to_all.25 = s32[8,16,2]{0,2,1:T(2,128)S(1)} all-to-all(s32[8,16,2]{0,2,1:T(2,128)S(1)} %copy.34), channel_id=1, replica_groups=mesh['group'=8,'member'=16] {'member'}, dimensions={1} | all-to-all | bytes 2048 | tf_op jit(solution)/shard_map/all_to_all | solution.py:91
  1131.1 0.1 copy.35
  1131.2 0.1 copy.36
  1131.3 0.1 sub.7
  1131.5 0.0 copy-done.6
  1131.5 0.5 fusion.26
  1132.0 0.1 reshape_transpose_transpose_reshape_reshape_reshape.3
  1132.0 22.3 all_to_all.26
  1154.4 0.2 fusion.27
  1154.6 0.1 copy.39
  1154.7 9.1 all_to_all.27
  1163.9 0.1 mul.160
  1164.0 0.0 copy-start.4
  1164.0 0.0 copy-start.5
  1164.0 0.0 collective-permute-done.3
  1164.0 13.8 multiply_reduce_fusion.1
  1177.8 0.0 copy-done.4
  1177.9 0.0 copy-done.5
  1177.9 11.5 fusion.47
  1189.4 0.3 collective-permute-start.4
  1189.6 269.5 %collective-permute-done.4 = f32[1536,2048]{1,0:T(8,128)S(1)} collective-permute-done((f32[1536,2048]{1,0:T(8,128)}, f32[1536,2048]{1,0:T(8,128)S(1)}, u32[]{:S(2)}, u32[]{:S(2)}) %collective-permute-start.4) | collective-permute-done | bytes 12582944 | tf_op jit(solution)/shard_map/ppermute | solution.py:67
  1459.2 6.0 add.109
  1465.2 1.2 collective-permute-start.5
  1466.4 269.2 %collective-permute-done.5 = f32[1536,2048]{1,0:T(8,128)} collective-permute-done((f32[1536,2048]{1,0:T(8,128)S(1)}, f32[1536,2048]{1,0:T(8,128)}, u32[]{:S(2)}, u32[]{:S(2)}) %collective-permute-start.5) | collective-permute-done | bytes 12582944 | tf_op jit(solution)/shard_map/ppermute | solution.py:67
  1735.6 6.0 add.110
  1741.6 0.0 copy-start.3
  1741.7 0.3 collective-permute-start.6
  1742.0 4.1 copy-done.3
  1746.1 263.5 %collective-permute-done.6 = f32[1536,2048]{1,0:T(8,128)} collective-permute-done((f32[1536,2048]{1,0:T(8,128)S(1)}, f32[1536,2048]{1,0:T(8,128)}, u32[]{:S(2)}, u32[]{:S(2)}) %collective-permute-start.6) | collective-permute-done | bytes 12582944 | tf_op jit(solution)/shard_map/ppermute | solution.py:67
  2009.6 15.2 add.111
  2024.8 0.9 collective-permute-start.7
  2025.8 267.7 %collective-permute-done.7 = f32[1536,2048]{1,0:T(8,128)} collective-permute-done((f32[1536,2048]{1,0:T(8,128)}, f32[1536,2048]{1,0:T(8,128)}, u32[]{:S(2)}, u32[]{:S(2)}) %collective-permute-start.7) | collective-permute-done | bytes 12582944 | tf_op jit(solution)/shard_map/ppermute | solution.py:67
  2293.5 13.8 multiply_reduce_fusion
  2307.4 9.7 add_convert_fusion
  (26 shorter events, 0.1 us)
Async XLA Ops:
  0.0 13.5 copy-start
  26.9 272.0 %collective-permute-start = (f32[1536,2048]{1,0:T(8,128)}, f32[1536,2048]{1,0:T(8,128)S(1)}, u32[]{:S(2)}, u32[]{:S(2)}) collective-permute-start(f32[1536,2048]{1,0:T(8,128)} %fusion.14), channel_id=1, source_target_pairs={{0,1},{1,0},{2,3},{3,2},{4,5},{5,4},{6,7},{7,6},{8,9},{9,8},{10,11... | collective-permute-start | bytes 37748744 | tf_op jit(solution)/shard_map/ppermute | solution.py:67
  304.9 272.3 %collective-permute-start.1 = (f32[1536,2048]{1,0:T(8,128)S(1)}, f32[1536,2048]{1,0:T(8,128)}, u32[]{:S(2)}, u32[]{:S(2)}) collective-permute-start(f32[1536,2048]{1,0:T(8,128)S(1)} %add.96), channel_id=1, source_target_pairs={{0,2},{1,3},{2,0},{3,1},{4,6},{5,7},{6,4},{7,5},{8,10},{9,11},{10,... | collective-permute-start | bytes 37748744 | tf_op jit(solution)/shard_map/ppermute | solution.py:67
  583.3 277.6 %copy-start.7 = (s32[96,1]{0,1:T(1,128)S(1)}, s32[96,1]{0,1:T(1,128)}, u32[]{:S(2)}) copy-start(s32[96,1]{0,1:T(1,128)} %param.12) | copy-start | bytes 1156
  583.3 277.6 %copy-start.2 = (s32[128]{0:T(128)S(1)}, s32[128]{0:T(128)}, u32[]{:S(2)}) copy-start(s32[128]{0:T(128)} %param.14) | copy-start | bytes 1540
  583.3 279.0 %copy-start.8 = (s32[96]{0:T(128)S(1)}, s32[96]{0:T(128)}, u32[]{:S(2)}) copy-start(s32[96]{0:T(128)} %param.13) | copy-start | bytes 1156
  583.3 548.2 %copy-start.6 = (bf16[2048,256]{1,0:T(8,128)(2,1)S(1)}, bf16[2048,256]{1,0:T(8,128)(2,1)}, u32[]{:S(2)}) copy-start(bf16[2048,256]{1,0:T(8,128)(2,1)} %param.15) | copy-start | bytes 3145732
  583.3 269.6 %collective-permute-start.2 = (f32[1536,2048]{1,0:T(8,128)S(1)}, f32[1536,2048]{1,0:T(8,128)S(1)}, u32[]{:S(2)}, u32[]{:S(2)}) collective-permute-start(f32[1536,2048]{1,0:T(8,128)S(1)} %add.97), channel_id=1, source_target_pairs={{0,4},{1,5},{2,6},{3,7},{4,0},{5,1},{6,2},{7,3},{8,12},{9,13},{10,... | collective-permute-start | bytes 37748744 | tf_op jit(solution)/shard_map/ppermute | solution.py:67
  858.3 305.7 %collective-permute-start.3 = (f32[1536,2048]{1,0:T(8,128)}, f32[1536,2048]{1,0:T(8,128)}, u32[]{:S(2)}, u32[]{:S(2)}) collective-permute-start(f32[1536,2048]{1,0:T(8,128)} %add.98), channel_id=1, source_target_pairs={{0,8},{1,9},{2,10},{3,11},{4,12},{5,13},{6,14},{7,15},{8,0},{9,1},... | collective-permute-start | bytes 37748744 | tf_op jit(solution)/shard_map/ppermute | solution.py:67
  1164.0 13.9 copy-start.4
  1164.0 13.9 copy-start.5
  1189.4 269.8 %collective-permute-start.4 = (f32[1536,2048]{1,0:T(8,128)}, f32[1536,2048]{1,0:T(8,128)S(1)}, u32[]{:S(2)}, u32[]{:S(2)}) collective-permute-start(f32[1536,2048]{1,0:T(8,128)} %fusion.47), channel_id=1, source_target_pairs={{0,1},{1,0},{2,3},{3,2},{4,5},{5,4},{6,7},{7,6},{8,9},{9,8},{10,11... | collective-permute-start | bytes 37748744 | tf_op jit(solution)/shard_map/ppermute | solution.py:67
  1465.2 270.4 %collective-permute-start.5 = (f32[1536,2048]{1,0:T(8,128)S(1)}, f32[1536,2048]{1,0:T(8,128)}, u32[]{:S(2)}, u32[]{:S(2)}) collective-permute-start(f32[1536,2048]{1,0:T(8,128)S(1)} %add.109), channel_id=1, source_target_pairs={{0,2},{1,3},{2,0},{3,1},{4,6},{5,7},{6,4},{7,5},{8,10},{9,11},{10,... | collective-permute-start | bytes 37748744 | tf_op jit(solution)/shard_map/ppermute | solution.py:67
  1741.6 4.5 copy-start.3
  1741.7 267.9 %collective-permute-start.6 = (f32[1536,2048]{1,0:T(8,128)S(1)}, f32[1536,2048]{1,0:T(8,128)}, u32[]{:S(2)}, u32[]{:S(2)}) collective-permute-start(f32[1536,2048]{1,0:T(8,128)S(1)} %add.110), channel_id=1, source_target_pairs={{0,4},{1,5},{2,6},{3,7},{4,0},{5,1},{6,2},{7,3},{8,12},{9,13},{10,... | collective-permute-start | bytes 37748744 | tf_op jit(solution)/shard_map/ppermute | solution.py:67
  2009.6 297.7 %slice-start = ((s8[12582912]{0:T(1024)(128)(4,1)}), s8[4194304]{0:T(1024)(128)(4,1)S(1)}, s32[]{:S(2)}) async-start(s8[12582912]{0:T(1024)(128)(4,1)} %bitcast.51), calls=%async_computation.4 | async-start | bytes 8388608
  2009.6 297.7 %slice-start.1 = ((s8[12582912]{0:T(1024)(128)(4,1)}), s8[4194304]{0:T(1024)(128)(4,1)S(1)}, s32[]{:S(2)}) async-start(s8[12582912]{0:T(1024)(128)(4,1)} %bitcast.51), calls=%async_computation.5 | async-start | bytes 8388608
  2009.6 297.7 %slice-start.3 = ((s8[6291456]{0:T(1024)(128)(4,1)}), s8[4194304]{0:T(1024)(128)(4,1)S(1)}, s32[]{:S(2)}) async-start(s8[6291456]{0:T(1024)(128)(4,1)} %bitcast.53), calls=%async_computation.7 | async-start | bytes 8388608
  2024.8 282.5 %slice-start.2 = ((s8[12582912]{0:T(1024)(128)(4,1)}), s8[4194304]{0:T(1024)(128)(4,1)S(1)}, s32[]{:S(2)}) async-start(s8[12582912]{0:T(1024)(128)(4,1)} %bitcast.51), calls=%async_computation.6 | async-start | bytes 8388608
  2024.8 282.5 %slice-start.4 = ((s8[6291456]{0:T(1024)(128)(4,1)}), s8[2097152]{0:T(1024)(128)(4,1)S(1)}, s32[]{:S(2)}) async-start(s8[6291456]{0:T(1024)(128)(4,1)} %bitcast.53), calls=%async_computation.8 | async-start | bytes 4194304
  2024.8 268.7 %collective-permute-start.7 = (f32[1536,2048]{1,0:T(8,128)}, f32[1536,2048]{1,0:T(8,128)}, u32[]{:S(2)}, u32[]{:S(2)}) collective-permute-start(f32[1536,2048]{1,0:T(8,128)} %add.111), channel_id=1, source_target_pairs={{0,8},{1,9},{2,10},{3,11},{4,12},{5,13},{6,14},{7,15},{8,0},{9,1},... | collective-permute-start | bytes 37748744 | tf_op jit(solution)/shard_map/ppermute | solution.py:67
  2307.3 9.8 copy-start.1
